TPU v7x, 32 devices: a whole 2x2x4 slice. The times are simulated.
32 devices in a mesh: space: 4 (over y, x), vel: 8 (over z, core).
Axes of the slice: x: 2, y: 2, z: 4, core: 2. Of those that a mesh axis runs over, the one named last changes fastest.
Arguments:
- distribution: float32 [256, 64, 4096], P('space', None, 'vel'), may hold values from -6 to 6
- inverse_jacobian: float32 [256, 3, 3], P('space'), may hold values from -1 to 1
- density: float32 [256, 64], P('space'), may hold values from 1 to 10
- collision_blocks: float32 [32, 6, 128, 128], replicated, may hold values from -0.21875 to 0.21875
- block_columns: int32 [32, 6], replicated, may hold values from 0 to 31, as said below
- send_lists: int32 [4, 4, 48], P('space'), may hold values from 0 to 383, as said below
- exterior_faces: int32 [256, 6], P('space'), may hold values from 0 to 576, as said below
Outputs:
- advanced: float32 [256, 64, 4096], P('space', None, 'vel')
Inputs may be any that keep to these rules, and one draw needn't show every extreme that they name: `block_columns`: each row b lists 6 different block columns, the first being b itself. send_lists[q, p] holds different faces (6 e + s, e local to q) in its first slots and 0 in the slots after them; send_lists[p, p] is all 0. Every used slot is read by exactly one face of partition p, and slots after the used ones are read by none. `exterior_faces`: an entry below 384 names a face 6 e + s of the partition's own elements; 384 + q * 48 + j names slot j of the list partition q sends to this partition; 576 marks a wall, whose exterior trace is zero. Exactly 32 faces of each partition are walls.
All inputs are finite; a program needn't handle non-finite values.
Results may differ from a plain program's by a relative error of at most 0.0003.
Values sent between devices are 32-bit elements; how exact they have to be, the bound alone decides.
No kernel may reach another device: no remote copies, remote signals or barrier semaphores. Data moves between devices by JAX's collectives and lax.ppermute only.
A program may use at most 256 MiB of HBM per device.

v0:
```python
import jax
import jax.numpy as jnp
import numpy as np
from jax import lax
from jax.sharding import PartitionSpec as P

VG = 16
TIME_STEP = 0.03
LIFT_SCALE = 6.0


def lagrange_derivative():
    points = np.array([-1.0, -1.0 / np.sqrt(5.0), 1.0 / np.sqrt(5.0), 1.0])
    barycentric = np.ones(4)
    for column in range(4):
        for second in range(4):
            if second != column:
                barycentric[column] = barycentric[column] / (points[column] - points[second])
    matrix = np.zeros((4, 4))
    for row_node in range(4):
        for col_node in range(4):
            if row_node != col_node:
                matrix[row_node, col_node] = (
                    barycentric[col_node]
                    / barycentric[row_node]
                    / (points[row_node] - points[col_node])
                )
        matrix[row_node, row_node] = -np.sum(matrix[row_node])
    return matrix


def derivative_stack():
    single = lagrange_derivative()
    identity = np.eye(4)
    stacked = np.concatenate(
        [
            np.kron(np.kron(single, identity), identity),
            np.kron(np.kron(identity, single), identity),
            np.kron(np.kron(identity, identity), single),
        ],
        0,
    )
    return jnp.asarray(stacked, dtype=jnp.float32)


def grid_velocities(first_id, amount):
    velocity_id = first_id + jnp.arange(amount, dtype=jnp.int32)
    components = [velocity_id // (VG * VG), velocity_id // VG % VG, velocity_id % VG]
    return [
        3.0 * ((2.0 * component.astype(jnp.float32) + 1.0) / VG - 1.0) for component in components
    ]


def face_speeds(inverse_jacobian, velocity_x, velocity_y, velocity_z):
    return (
        inverse_jacobian[:, :, 0, None] * velocity_x[None, None, :]
        + inverse_jacobian[:, :, 1, None] * velocity_y[None, None, :]
        + inverse_jacobian[:, :, 2, None] * velocity_z[None, None, :]
    )


def face_values(node_field):
    node_cube = node_field.reshape(node_field.shape[0], 4, 4, 4, node_field.shape[2])
    face_list = [
        node_cube[:, 0],
        node_cube[:, 3],
        node_cube[:, :, 0],
        node_cube[:, :, 3],
        node_cube[:, :, :, 0],
        node_cube[:, :, :, 3],
    ]
    return jnp.stack(face_list, 1).reshape(node_field.shape[0], 6, 16, node_field.shape[2])


def lift_faces(face_flux):
    elements = face_flux.shape[0]
    columns = face_flux.shape[3]
    blocks = face_flux.reshape(elements, 6, 4, 4, columns)
    summed = jnp.zeros((elements, 4, 4, 4, columns), jnp.float32)
    for face_id in range(6):
        direction = face_id // 2
        placed = jnp.expand_dims(blocks[:, face_id], 1 + direction)
        padding = [(0, 0), (0, 0), (0, 0), (0, 0), (0, 0)]
        padding[1 + direction] = (0, 3) if face_id % 2 == 0 else (3, 0)
        summed = summed + jnp.pad(placed, padding)
    return summed.reshape(elements, 64, columns)


def advection(node_field, speeds, interior, outside):
    stacked = derivative_stack()
    derived = jnp.einsum("mn,env->emv", stacked, node_field, precision=lax.Precision.HIGHEST)
    derived = derived.reshape(node_field.shape[0], 3, node_field.shape[1], node_field.shape[2])
    volume = -(
        speeds[:, 0, None, :] * derived[:, 0]
        + speeds[:, 1, None, :] * derived[:, 1]
        + speeds[:, 2, None, :] * derived[:, 2]
    )
    face_signs = jnp.asarray(np.array([-1.0, 1.0, -1.0, 1.0, -1.0, 1.0]), dtype=jnp.float32)
    normal = jnp.repeat(speeds, 2, axis=1) * face_signs[None, :, None]
    weight = LIFT_SCALE * jnp.minimum(normal, 0.0)
    face_flux = weight[:, :, None, :] * (interior - outside)
    return volume + lift_faces(face_flux)


def collide(node_block, collision_blocks, block_columns):
    block_rows = collision_blocks.shape[0]
    block_count = collision_blocks.shape[1]
    width = collision_blocks.shape[2]
    flat_rows = node_block.reshape(-1, node_block.shape[-1])
    outputs = []
    for block_id in range(block_rows):
        total = jnp.zeros((flat_rows.shape[0], width), jnp.float32)
        for slot in range(block_count):
            start = block_columns[block_id, slot] * width
            piece = lax.dynamic_slice_in_dim(flat_rows, start, width, 1)
            total = total + lax.dot_general(
                piece,
                collision_blocks[block_id, slot],
                (((1,), (1,)), ((), ())),
                precision=lax.Precision.HIGHEST,
                preferred_element_type=jnp.float32,
            )
        outputs.append(total)
    applied = jnp.concatenate(outputs, 1).reshape(node_block.shape)
    return applied - node_block


def body(
    distribution,
    inverse_jacobian,
    density,
    collision_blocks,
    block_columns,
    send_lists,
    exterior_faces,
):
    vel_id = lax.axis_index("vel")
    span_local = distribution.shape[2]
    velocity = grid_velocities(vel_id * span_local, span_local)
    speeds = face_speeds(inverse_jacobian, velocity[0], velocity[1], velocity[2])
    send_rows = send_lists[0]
    lookup = exterior_faces.reshape(-1)

    def advect(node_field):
        interior = face_values(node_field)
        table_own = interior.reshape(-1, 16, span_local)
        outgoing = jnp.take(table_own, send_rows, axis=0)
        incoming = lax.all_to_all(outgoing, "space", split_axis=0, concat_axis=0, tiled=True)
        face_table = jnp.concatenate(
            [
                table_own,
                incoming.reshape(-1, 16, span_local),
                jnp.zeros((1, 16, span_local), jnp.float32),
            ],
            0,
        )
        outside = jnp.take(face_table, lookup, axis=0).reshape(interior.shape)
        return advection(node_field, speeds, interior, outside)

    def on_nodes(node_block):
        change = collide(node_block, collision_blocks, block_columns)
        returned = lax.all_to_all(change, "vel", split_axis=2, concat_axis=1, tiled=True)
        return (returned, node_block, change)

    def to_nodes(node_field):
        return on_nodes(lax.all_to_all(node_field, "vel", split_axis=1, concat_axis=2, tiled=True))

    scaling = density[:, :, None]
    flow_zero = advect(distribution)
    back_zero, nodes_zero, change_zero = to_nodes(distribution)
    first_section = distribution + TIME_STEP * (flow_zero + scaling * back_zero)
    flow_one = advect(first_section)
    back_one = to_nodes(first_section)[0]
    return 0.5 * distribution + 0.5 * (first_section + TIME_STEP * (flow_one + scaling * back_one))


def solution(mesh):
    in_specs = (
        P("space", None, "vel"),
        P("space", None, None),
        P("space", None),
        P(),
        P(),
        P("space", None, None),
        P("space", None),
    )
    out_specs = P("space", None, "vel")
    return jax.shard_map(body, mesh=mesh, in_specs=in_specs, out_specs=out_specs, check_vma=False)
```

profile of v0, /device:TPU:0, one launch (start us, length us, event | category | flops | bytes accessed | tf_op | source)
XLA Modules:
  0.0 1381.4 jit_solution(17776754912822584726)
XLA Ops:
  156.2 15.2 %copy.198 = f32[64,6,4,4,512]{4,3,2,1,0:T(4,128)} copy(f32[64,6,4,4,512]{4,0,3,2,1:T(8,128)S(1)} %fusion.37) | data formatting | bytes 25165824 | tf_op jit(solution)/shard_map/stack | solution.py:72
  171.4 14.7 %reshape_reshape.6 = f32[384,16,512]{2,1,0:T(8,128)} reshape(f32[64,6,4,4,512]{4,3,2,1,0:T(4,128)} %copy.198) | data formatting | bytes 25165824 | tf_op jit(solution)/shard_map/reshape;reshape | solution.py:146
  369.0 15.4 %reshape.653 = f32[8,1,262144]{2,1,0:T(1,128)} reshape(f32[4096,8,64]{2,1,0:T(8,128)} %bitcast.1762) | data formatting | bytes 16777216
  390.8 25.1 %fusion.1745 = f32[192,64,512]{2,0,1:T(8,128)} fusion(f32[192,64,1]{0,1,2:T(8,128)S(1)} %copy-done.21, f32[64,64,512]{2,1,0:T(8,128)} %param.15), kind=kOutput, calls=%fused_computation.2140 | convolution fusion | flops 4831838208 | bytes 33603584 | tf_op jit(solution)/shard_map/mn,env->emv/dot_general | solution.py:91
  416.0 18.2 %fusion.1731 = (f32[64,1,64,512]{3,2,1,0:T(8,128)}, f32[64,1,64,512]{3,2,1,0:T(8,128)}, f32[64,1,64,512]{3,2,1,0:T(8,128)}) fusion(f32[64,3,64,512]{3,2,1,0:T(8,128)} %bitcast.1752), kind=kLoop, calls=%fused_computation.2126 | loop fusion | bytes 50331648 | tf_op jit(solution)/shard_map/slice | solution.py:94
  434.2 16.1 %maximum_maximum_fusion = f32[577,16,512]{2,1,0:T(8,128)} fusion(f32[192,16,512]{2,1,0:T(8,128)} %bitcast.18, f32[384,16,512]{2,1,0:T(8,128)} %reshape_reshape.6, f32[577]{0:T(1024)S(1)} %pad.59.clone), kind=kLoop, calls=%fused_computation.4 | loop fusion | flops 9453568 | bytes 37783812 | tf_op jit(solution)/shard_map/concatenate | solution.py:149
  473.1 14.5 %reshape.590 = f32[64,6,4,4,512]{4,3,2,1,0:T(4,128)} reshape(f32[384,16,512]{2,1,0:T(8,128)} %broadcast_select_fusion.1) | data formatting | bytes 25165824 | tf_op jit(solution)/shard_map/reshape | solution.py:157
  487.5 13.9 %fusion.1 = f32[64,6,4,4,512]{4,0,3,2,1:T(8,128)S(1)} fusion(f32[64,6,4,4,512]{4,0,3,2,1:T(8,128)} %copy-done.5, f32[64,6,4,4,512]{4,3,2,1,0:T(4,128)} %reshape.590, f32[64,6,512]{2,0,1:T(8,128)S(1)} %fusion.106), kind=kLoop, calls=%fused_computation.9 | loop fusion | flops 6291456 | bytes 38535168 | tf_op jit(solution)/shard_map/mul | solution.py:101
  523.1 50.5 %all-to-all-done.2 = f32[8,1,262144]{2,1,0:T(1,128)} async-done(((f32[8,1,262144]{2,1,0:T(1,128)}), f32[8,1,262144]{2,1,0:T(1,128)}, u32[]{:S(2)}, u32[]{:S(2)}) %all-to-all-start.2) | async-done | bytes 8388640 | tf_op jit(solution)/shard_map/all_to_all | solution.py:162
  574.2 26.2 %reduce = f32[8,262144]{1,0:T(8,128)} reduce(f32[8,1,262144]{2,1,0:T(1,128)} %all-to-all-done.2, f32[]{:T(128)} %broadcast.344), dimensions={1}, to_apply=%all_to_all.63.reduce_sub_computation | reduce | bytes 16777220 | tf_op jit(solution)/shard_map/all_to_all | solution.py:162
  600.5 15.7 %reshape.654 = f32[4096,8,64]{2,1,0:T(8,128)} reshape(f32[8,262144]{1,0:T(8,128)} %reduce) | data formatting | bytes 16777216
  628.9 42.2 %fusion.27 = f32[64,64,512]{2,0,1:T(8,128)} fusion(f32[64,1,64,512]{3,2,1,0:T(8,128)} %get-tuple-element.12, f32[64,1,64,512]{3,2,1,0:T(8,128)} %get-tuple-element.11, f32[64,1,64,512]{3,2,1,0:T(8,128)} %get-tuple-element.10, f32[64,8,8,512]{3,0,1,2:T(8,128)} %copy.210, f32[64,4,4,4,512]{4,0,3,2,1:T(8,128)} %copy.204, f32[64,64]{0,1:T(8,128)S(1)} %copy.205, ...), kind=kLoop, calls=%fused_computation.43 | loop fusion | flops 23068672 | bytes 59129856 | tf_op jit(solution)/shard_map/add | solution.py:171
  686.2 15.2 %copy.220 = f32[64,6,4,4,512]{4,3,2,1,0:T(4,128)} copy(f32[64,6,4,4,512]{4,0,3,2,1:T(8,128)S(1)} %fusion.33) | data formatting | bytes 25165824 | tf_op jit(solution)/shard_map/stack | solution.py:72
  701.4 14.7 %reshape_reshape.7 = f32[384,16,512]{2,1,0:T(8,128)} reshape(f32[64,6,4,4,512]{4,3,2,1,0:T(4,128)} %copy.220) | data formatting | bytes 25165824 | tf_op jit(solution)/shard_map/reshape;reshape | solution.py:146
  730.3 129.6 %all-to-all-done.4 = f32[64,64,512]{2,0,1:T(8,128)} async-done(((f32[64,64,512]{2,0,1:T(8,128)}), f32[64,64,512]{2,0,1:T(8,128)}, u32[]{:S(2)}, u32[]{:S(2)}) %all-to-all-start.4) | async-done | bytes 8388640 | tf_op jit(solution)/shard_map/all_to_all | solution.py:166
  1074.9 15.5 %reshape.655 = f32[8,1,262144]{2,1,0:T(1,128)} reshape(f32[4096,8,64]{2,1,0:T(8,128)} %bitcast.1764) | data formatting | bytes 16777216
  1095.5 29.9 %fusion.31 = f32[64,512,192]{1,2,0:T(8,128)} fusion(f32[192,64,1]{0,1,2:T(8,128)S(1)} %copy-done.22, f32[64,64,512]{2,0,1:T(8,128)} %fusion.27), kind=kOutput, calls=%fused_computation.55 | convolution fusion | flops 4831838208 | bytes 33603584 | tf_op jit(solution)/shard_map/mn,env->emv/dot_general | solution.py:91
  1125.4 18.3 %fusion.1730 = (f32[64,1,64,512]{3,2,1,0:T(8,128)}, f32[64,1,64,512]{3,2,1,0:T(8,128)}, f32[64,1,64,512]{3,2,1,0:T(8,128)}) fusion(f32[64,3,64,512]{3,2,1,0:T(8,128)} %bitcast.1753), kind=kLoop, calls=%fused_computation.2125 | loop fusion | bytes 50331648 | tf_op jit(solution)/shard_map/slice | solution.py:94
  1143.8 16.1 %maximum_maximum_fusion.1 = f32[577,16,512]{2,1,0:T(8,128)} fusion(f32[192,16,512]{2,1,0:T(8,128)} %bitcast.429, f32[384,16,512]{2,1,0:T(8,128)} %reshape_reshape.7, f32[577]{0:T(1024)S(1)} %copy-done.24), kind=kLoop, calls=%fused_computation.5 | loop fusion | flops 9453568 | bytes 37783812 | tf_op jit(solution)/shard_map/concatenate | solution.py:149
  1182.6 14.6 %reshape.597 = f32[64,6,4,4,512]{4,3,2,1,0:T(4,128)} reshape(f32[384,16,512]{2,1,0:T(8,128)} %broadcast_select_fusion) | data formatting | bytes 25165824 | tf_op jit(solution)/shard_map/reshape | solution.py:157
  1230.8 48.6 %all-to-all-done.5 = f32[8,1,262144]{2,1,0:T(1,128)} async-done(((f32[8,1,262144]{2,1,0:T(1,128)}), f32[8,1,262144]{2,1,0:T(1,128)}, u32[]{:S(2)}, u32[]{:S(2)}) %all-to-all-start.5) | async-done | bytes 8388640 | tf_op jit(solution)/shard_map/all_to_all | solution.py:162
  1279.4 26.7 %reduce.1 = f32[8,262144]{1,0:T(8,128)} reduce(f32[8,1,262144]{2,1,0:T(1,128)} %all-to-all-done.5, f32[]{:T(128)} %broadcast.344), dimensions={1}, to_apply=%all_to_all.72.reduce_sub_computation | reduce | bytes 16777220 | tf_op jit(solution)/shard_map/all_to_all | solution.py:162
  1306.1 15.7 %reshape.656 = f32[4096,8,64]{2,1,0:T(8,128)} reshape(f32[8,262144]{1,0:T(8,128)} %reduce.1) | data formatting | bytes 16777216
  1334.6 38.3 %fusion.12 = f32[64,64,512]{2,0,1:T(8,128)S(1)} fusion(f32[64,64,512]{2,0,1:T(8,128)} %fusion.27, f32[64,1,64,512]{3,2,1,0:T(8,128)} %get-tuple-element.9, f32[64,1,64,512]{3,2,1,0:T(8,128)} %get-tuple-element.8, f32[64,1,64,512]{3,2,1,0:T(8,128)} %get-tuple-element.6, f32[64,8,8,512]{3,0,1,2:T(8,128)} %copy.230, f32[64,4,4,4,512]{4,0,3,2,1:T(8,128)} %copy.226, ...), kind=kLoop, calls=%fused_computation.24 | loop fusion | flops 27262976 | bytes 67518464 | tf_op jit(solution)/shard_map/add | solution.py:174
  (561 shorter events, 607.5 us)
Async XLA Ops:
  11.6 134.2 %copy-start.30 = (s32[1,4,48]{2,1,0:T(4,128)S(1)}, s32[1,4,48]{2,1,0:T(4,128)}, u32[]{:S(2)}) copy-start(s32[1,4,48]{2,1,0:T(4,128)} %param.20) | copy-start | bytes 2308
  11.6 191.0 %all-to-all-start.1 = ((f32[64,64,512]{2,0,1:T(8,128)}), f32[64,64,512]{2,0,1:T(8,128)}, u32[]{:S(2)}, u32[]{:S(2)}) async-start(f32[64,64,512]{2,0,1:T(8,128)} %copy.231), calls=%async_computation.1 | async-start | bytes 16777216 | tf_op jit(solution)/shard_map/all_to_all | solution.py:166
  202.6 181.9 %all-to-all-start = ((f32[4,48,16,512]{3,2,1,0:T(8,128)}), f32[4,48,16,512]{3,2,1,0:T(8,128)}, u32[]{:S(2)}, u32[]{:S(2)}) async-start(f32[4,48,16,512]{3,2,1,0:T(8,128)} %broadcast_select_fusion.3), calls=%async_computation | async-start | bytes 12582912 | tf_op jit(solution)/shard_map/all_to_all | solution.py:148
  208.1 30.2 %slice-start = ((s8[12582912]{0:T(1024)(128)(4,1)}), s8[4194304]{0:T(1024)(128)(4,1)S(1)}, s32[]{:S(2)}) async-start(s8[12582912]{0:T(1024)(128)(4,1)} %bitcast.1766), calls=%async_computation.6 | async-start | bytes 8388608
  208.1 30.2 %slice-start.1 = ((s8[12582912]{0:T(1024)(128)(4,1)}), s8[4194304]{0:T(1024)(128)(4,1)S(1)}, s32[]{:S(2)}) async-start(s8[12582912]{0:T(1024)(128)(4,1)} %bitcast.1766), calls=%async_computation.7 | async-start | bytes 8388608
  216.5 117.9 %copy-start = (f32[64,8,8,512]{3,2,1,0:T(8,128)}, f32[64,8,8,512]{3,2,1,0:T(8,128)S(1)}, u32[]{:S(2)}) copy-start(f32[64,8,8,512]{3,2,1,0:T(8,128)S(1)} %copy.207) | copy-start | bytes 25165828
  216.5 21.8 %slice-start.2 = ((s8[12582912]{0:T(1024)(128)(4,1)}), s8[4194304]{0:T(1024)(128)(4,1)S(1)}, s32[]{:S(2)}) async-start(s8[12582912]{0:T(1024)(128)(4,1)} %bitcast.1766), calls=%async_computation.8 | async-start | bytes 8388608
  384.5 189.2 %all-to-all-start.2 = ((f32[8,1,262144]{2,1,0:T(1,128)}), f32[8,1,262144]{2,1,0:T(1,128)}, u32[]{:S(2)}, u32[]{:S(2)}) async-start(f32[8,1,262144]{2,1,0:T(1,128)} %reshape.653), calls=%async_computation.2 | async-start | bytes 16777216 | tf_op jit(solution)/shard_map/all_to_all | solution.py:162
  390.0 238.9 %copy-start.19 = (f32[64,64]{0,1:T(8,128)}, f32[64,64]{0,1:T(8,128)S(1)}, u32[]{:S(2)}) copy-start(f32[64,64]{0,1:T(8,128)S(1)} %copy.205) | copy-start | bytes 49156
  390.3 43.9 %copy-start.23 = (f32[577]{0:T(1024)}, f32[577]{0:T(1024)S(1)}, u32[]{:S(2)}) copy-start(f32[577]{0:T(1024)S(1)} %pad.59.clone) | copy-start | bytes 6928
  390.7 96.9 %copy-start.10 = (f32[64,6,512]{2,0,1:T(8,128)}, f32[64,6,512]{2,0,1:T(8,128)S(1)}, u32[]{:S(2)}) copy-start(f32[64,6,512]{2,0,1:T(8,128)S(1)} %fusion.106) | copy-start | bytes 2359300
  390.7 59.6 %copy-start.26 = (s32[1024]{0:T(1024)}, s32[1024]{0:T(1024)S(1)}, u32[]{:S(2)}) copy-start(s32[1024]{0:T(1024)S(1)} %pad_clamp_fusion) | copy-start | bytes 12292
  390.7 71.9 %copy-start.31 = (pred[384]{0:T(512)(128)(4,1)}, pred[384]{0:T(512)(128)(4,1)S(1)}, u32[]{:S(2)}) copy-start(pred[384]{0:T(512)(128)(4,1)S(1)} %compare_and_fusion) | copy-start | bytes 1156
  390.8 238.1 %copy-start.13 = (f32[64,512]{1,0:T(8,128)}, f32[64,512]{1,0:T(8,128)S(1)}, u32[]{:S(2)}) copy-start(f32[64,512]{1,0:T(8,128)S(1)} %get-tuple-element.23) | copy-start | bytes 393220
  390.8 238.1 %copy-start.15 = (f32[64,512]{1,0:T(8,128)}, f32[64,512]{1,0:T(8,128)S(1)}, u32[]{:S(2)}) copy-start(f32[64,512]{1,0:T(8,128)S(1)} %get-tuple-element.24) | copy-start | bytes 393220
  390.8 238.1 %copy-start.17 = (f32[64,512]{1,0:T(8,128)}, f32[64,512]{1,0:T(8,128)S(1)}, u32[]{:S(2)}) copy-start(f32[64,512]{1,0:T(8,128)S(1)} %get-tuple-element.25) | copy-start | bytes 393220
  671.0 188.8 %all-to-all-start.4 = ((f32[64,64,512]{2,0,1:T(8,128)}), f32[64,64,512]{2,0,1:T(8,128)}, u32[]{:S(2)}, u32[]{:S(2)}) async-start(f32[64,64,512]{2,0,1:T(8,128)} %fusion.27), calls=%async_computation.4 | async-start | bytes 16777216 | tf_op jit(solution)/shard_map/all_to_all | solution.py:166
  859.9 230.6 %all-to-all-start.3 = ((f32[4,48,16,512]{3,2,1,0:T(8,128)}), f32[4,48,16,512]{3,2,1,0:T(8,128)}, u32[]{:S(2)}, u32[]{:S(2)}) async-start(f32[4,48,16,512]{3,2,1,0:T(8,128)} %broadcast_select_fusion.2), calls=%async_computation.3 | async-start | bytes 12582912 | tf_op jit(solution)/shard_map/all_to_all | solution.py:148
  881.9 122.2 %copy-start.1 = (f32[64,8,8,512]{3,1,2,0:T(8,128)}, f32[64,8,8,512]{3,1,2,0:T(8,128)S(1)}, u32[]{:S(2)}) copy-start(f32[64,8,8,512]{3,1,2,0:T(8,128)S(1)} %copy.256) | copy-start | bytes 25165828
  881.9 49.8 %slice-start.3 = ((s8[12582912]{0:T(1024)(128)(4,1)}), s8[4194304]{0:T(1024)(128)(4,1)S(1)}, s32[]{:S(2)}) async-start(s8[12582912]{0:T(1024)(128)(4,1)} %bitcast.1768), calls=%async_computation.9 | async-start | bytes 8388608
  901.1 30.6 %slice-start.4 = ((s8[12582912]{0:T(1024)(128)(4,1)}), s8[4194304]{0:T(1024)(128)(4,1)S(1)}, s32[]{:S(2)}) async-start(s8[12582912]{0:T(1024)(128)(4,1)} %bitcast.1768), calls=%async_computation.10 | async-start | bytes 8388608
  1090.4 189.0 %all-to-all-start.5 = ((f32[8,1,262144]{2,1,0:T(1,128)}), f32[8,1,262144]{2,1,0:T(1,128)}, u32[]{:S(2)}, u32[]{:S(2)}) async-start(f32[8,1,262144]{2,1,0:T(1,128)} %reshape.655), calls=%async_computation.5 | async-start | bytes 16777216 | tf_op jit(solution)/shard_map/all_to_all | solution.py:162
  1125.4 18.3 %copy-start.24 = (f32[577]{0:T(1024)S(1)}, f32[577]{0:T(1024)}, u32[]{:S(2)}) copy-start(f32[577]{0:T(1024)} %copy-done.23) | copy-start | bytes 6928
  1143.8 16.1 %copy-start.27 = (s32[1024]{0:T(1024)S(1)}, s32[1024]{0:T(1024)}, u32[]{:S(2)}) copy-start(s32[1024]{0:T(1024)} %copy-done.26) | copy-start | bytes 12292
  (28 other events, 219.7 us)
where the time goes:
time: 1390 us; the launch traced here: 1380 us
  local copies, waits for them, and re-layouts  413 us (30%)
  matrix products  321 us (23%)
  other arithmetic  261 us (19%)
  waiting for transfers between devices  231 us (17%)
  between operations  123 us (9%)
  starting transfers between devices  33.1 us (2%)
    dot_general x384, matrix products, collide(): lax.dot_general(piece, collision_blocks[block_id, slot], (((1,), (1,)), (...  266 us
    all_to_all x2, waiting for transfers between devices, to_nodes(): lax.all_to_all(node_field, 'vel', split_axis=1, concat_axis=2, tiled=True)  131 us
    unnamed x114, local copies, waits for them, and re-layouts  107 us
    all_to_all x2, waiting for transfers between devices, on_nodes(): lax.all_to_all(change, 'vel', split_axis=2, concat_axis=1, tiled=True)  99.1 us
    dot_general x2, matrix products, advection(): jnp.einsum('mn,env->emv', stacked, node_field, precision=lax.Precision.HI...  55 us
    all_to_all x2, other arithmetic, on_nodes(): lax.all_to_all(change, 'vel', split_axis=2, concat_axis=1, tiled=True)  52.9 us
    add x1, other arithmetic, body(): first_section = distribution + TIME_STEP * (flow_zero + scaling * back_zero)  42.2 us
    add x1, other arithmetic, body(): 0.5 * distribution  38.3 us
  transfers between devices with their start and end apart: 6, of which 4 were waited for; matrix products, arithmetic and copies ran while one was open for 55% of the time, Pallas kernels for 0%

commit v1 on v0

--- a/solution.py
+++ b/solution.py
@@ -159,7 +159,10 @@
 
     def on_nodes(node_block):
         change = collide(node_block, collision_blocks, block_columns)
-        returned = lax.all_to_all(change, "vel", split_axis=2, concat_axis=1, tiled=True)
+        returned = jnp.concatenate(
+            lax.all_to_all(jnp.stack(jnp.split(change, lax.axis_size("vel"), axis=2)), "vel", 0, 0),
+            axis=1,
+        )
         return (returned, node_block, change)
 
     def to_nodes(node_field):

time: 1390 us -> 1290 us (0.928)
  local copies, waits for them, and re-layouts: 413 us -> 352 us
  other arithmetic: 261 us -> 224 us
    all_to_all x2 -> x0, other arithmetic: 52.9 us -> none  [on_nodes(): lax.all_to_all(change, 'vel', split_axis=2, concat_axis=1, tiled=True)]
    unnamed x114 -> x126, local copies, waits for them, and re-layouts: 107 us -> 78.2 us
    sub x2 -> x0, local copies, waits for them, and re-layouts: 26.7 us -> none  [collide(): return applied - node_block]
    all_to_all x3 -> x0, local copies, waits for them, and re-layouts: 26 us -> none  [on_nodes(): lax.all_to_all(change, 'vel', split_axis=2, concat_axis=1, tiled=True)]
  transfers between devices with their start and end apart: 6 -> 6, of which waited for: 4 -> 4; matrix products, arithmetic and copies ran while one was open for 55% -> 58% of each run, Pallas kernels for 0% -> 0%
where the time goes in v1:
time: 1290 us; the launch traced here: 1270 us
  local copies, waits for them, and re-layouts  352 us (27%)
  matrix products  313 us (24%)
  waiting for transfers between devices  231 us (18%)
  other arithmetic  224 us (17%)
  between operations  123 us (10%)
  starting transfers between devices  33 us (3%)
    dot_general x384, matrix products, collide(): lax.dot_general(piece, collision_blocks[block_id, slot], (((1,), (1,)), (...  258 us
    all_to_all x2, waiting for transfers between devices, to_nodes(): lax.all_to_all(node_field, 'vel', split_axis=1, concat_axis=2, tiled=True)  132 us
    all_to_all x2, waiting for transfers between devices, on_nodes(): lax.all_to_all(jnp.stack(jnp.split(change, lax.axis_size('vel'), axis=2))...  98.9 us
    unnamed x126, local copies, waits for them, and re-layouts  78.2 us
    dot_general x2, matrix products, advection(): jnp.einsum('mn,env->emv', stacked, node_field, precision=lax.Precision.HI...  55 us
    add x1, other arithmetic, body(): first_section = distribution + TIME_STEP * (flow_zero + scaling * back_zero)  52.3 us
    add x1, other arithmetic, body(): 0.5 * distribution  44.3 us
    slice x2, local copies, waits for them, and re-layouts, advection(): derived[:, 0]  36.6 us
  transfers between devices with their start and end apart: 6, of which 4 were waited for; matrix products, arithmetic and copies ran while one was open for 58% of the time, Pallas kernels for 0%

profile of v1, /device:TPU:0, one launch (start us, length us, event | category | flops | bytes accessed | tf_op | source)
XLA Modules:
  0.0 1274.8 jit_solution(3578454796269188615)
XLA Ops:
  0.0 11.6 copy.192
  155.9 15.2 %copy.159 = f32[64,6,4,4,512]{4,3,2,1,0:T(4,128)} copy(f32[64,6,4,4,512]{4,0,3,2,1:T(8,128)S(1)} %fusion.37) | data formatting | bytes 25165824 | tf_op jit(solution)/shard_map/stack | solution.py:72
  171.1 14.7 %reshape_reshape.6 = f32[384,16,512]{2,1,0:T(8,128)} reshape(f32[64,6,4,4,512]{4,3,2,1,0:T(4,128)} %copy.159) | data formatting | bytes 25165824 | tf_op jit(solution)/shard_map/reshape;reshape | solution.py:146
  344.5 11.3 bitcast_subtract_fusion.1
  380.2 25.1 %fusion.1761 = f32[192,64,512]{2,0,1:T(8,128)} fusion(f32[192,64,1]{0,1,2:T(8,128)S(1)} %copy-done.22, f32[64,64,512]{2,1,0:T(8,128)} %param.15), kind=kOutput, calls=%fused_computation.2174 | convolution fusion | flops 4831838208 | bytes 33603584 | tf_op jit(solution)/shard_map/mn,env->emv/dot_general | solution.py:91
  405.3 18.3 %fusion.1747 = (f32[64,1,64,512]{3,2,1,0:T(8,128)}, f32[64,1,64,512]{3,2,1,0:T(8,128)}, f32[64,1,64,512]{3,2,1,0:T(8,128)}) fusion(f32[64,3,64,512]{3,2,1,0:T(8,128)} %bitcast.1808), kind=kLoop, calls=%fused_computation.2160 | loop fusion | bytes 50331648 | tf_op jit(solution)/shard_map/slice | solution.py:94
  423.6 16.1 %maximum_maximum_fusion = f32[577,16,512]{2,1,0:T(8,128)} fusion(f32[192,16,512]{2,1,0:T(8,128)} %bitcast.18, f32[384,16,512]{2,1,0:T(8,128)} %reshape_reshape.6, f32[577]{0:T(1024)S(1)} %pad.59.clone), kind=kLoop, calls=%fused_computation.4 | loop fusion | flops 9453568 | bytes 37783812 | tf_op jit(solution)/shard_map/concatenate | solution.py:149
  439.7 12.3 gather_fusion.1
  462.5 14.5 %reshape.602 = f32[64,6,4,4,512]{4,3,2,1,0:T(4,128)} reshape(f32[384,16,512]{2,1,0:T(8,128)} %broadcast_select_fusion.1) | data formatting | bytes 25165824 | tf_op jit(solution)/shard_map/reshape | solution.py:157
  477.0 13.8 %fusion.1 = f32[64,6,4,4,512]{4,0,3,2,1:T(8,128)S(1)} fusion(f32[64,6,4,4,512]{4,0,3,2,1:T(8,128)} %copy-done.5, f32[64,6,4,4,512]{4,3,2,1,0:T(4,128)} %reshape.602, f32[64,6,512]{2,0,1:T(8,128)S(1)} %fusion.122), kind=kLoop, calls=%fused_computation.9 | loop fusion | flops 6291456 | bytes 38535168 | tf_op jit(solution)/shard_map/mul | solution.py:101
  512.5 50.6 %all-to-all-done.2 = f32[8,64,8,512]{3,2,1,0:T(8,128)} async-done(((f32[8,64,8,512]{3,2,1,0:T(8,128)}), f32[8,64,8,512]{3,2,1,0:T(8,128)}, u32[]{:S(2)}, u32[]{:S(2)}) %all-to-all-start.2) | async-done | bytes 8388640 | tf_op jit(solution)/shard_map/all_to_all | solution.py:163
  571.2 52.3 %fusion.27 = f32[64,64,512]{2,0,1:T(8,128)} fusion(f32[64,1,64,512]{3,2,1,0:T(8,128)} %get-tuple-element.12, f32[64,1,64,512]{3,2,1,0:T(8,128)} %get-tuple-element.11, f32[64,1,64,512]{3,2,1,0:T(8,128)} %get-tuple-element.10, f32[64,4,4,4,512]{4,0,3,2,1:T(8,128)} %copy.165, f32[64,64,512]{2,1,0:T(8,128)} %copy_bitcast_fusion.8, f32[64,64]{0,1:T(8,128)S(1)} %copy.166, ...), kind=kLoop, calls=%fused_computation.43 | loop fusion | flops 23068672 | bytes 59129856 | tf_op jit(solution)/shard_map/add | solution.py:174
  638.7 15.2 %copy.181 = f32[64,6,4,4,512]{4,3,2,1,0:T(4,128)} copy(f32[64,6,4,4,512]{4,0,3,2,1:T(8,128)S(1)} %fusion.33) | data formatting | bytes 25165824 | tf_op jit(solution)/shard_map/stack | solution.py:72
  653.9 14.7 %reshape_reshape.7 = f32[384,16,512]{2,1,0:T(8,128)} reshape(f32[64,6,4,4,512]{4,3,2,1,0:T(4,128)} %copy.181) | data formatting | bytes 25165824 | tf_op jit(solution)/shard_map/reshape;reshape | solution.py:146
  682.7 129.6 %all-to-all-done.4 = f32[64,64,512]{2,0,1:T(8,128)} async-done(((f32[64,64,512]{2,0,1:T(8,128)}), f32[64,64,512]{2,0,1:T(8,128)}, u32[]{:S(2)}, u32[]{:S(2)}) %all-to-all-start.4) | async-done | bytes 8388640 | tf_op jit(solution)/shard_map/all_to_all | solution.py:169
  1029.0 29.9 %fusion.31 = f32[64,512,192]{1,2,0:T(8,128)} fusion(f32[192,64,1]{0,1,2:T(8,128)S(1)} %copy-done.23, f32[64,64,512]{2,0,1:T(8,128)} %fusion.27), kind=kOutput, calls=%fused_computation.55 | convolution fusion | flops 4831838208 | bytes 33603584 | tf_op jit(solution)/shard_map/mn,env->emv/dot_general | solution.py:91
  1058.9 18.3 %fusion.1746 = (f32[64,1,64,512]{3,2,1,0:T(8,128)}, f32[64,1,64,512]{3,2,1,0:T(8,128)}, f32[64,1,64,512]{3,2,1,0:T(8,128)}) fusion(f32[64,3,64,512]{3,2,1,0:T(8,128)} %bitcast.1809), kind=kLoop, calls=%fused_computation.2159 | loop fusion | bytes 50331648 | tf_op jit(solution)/shard_map/slice | solution.py:94
  1077.2 16.1 %maximum_maximum_fusion.1 = f32[577,16,512]{2,1,0:T(8,128)} fusion(f32[192,16,512]{2,1,0:T(8,128)} %bitcast.436, f32[384,16,512]{2,1,0:T(8,128)} %reshape_reshape.7, f32[577]{0:T(1024)S(1)} %copy-done.25), kind=kLoop, calls=%fused_computation.5 | loop fusion | flops 9453568 | bytes 37783812 | tf_op jit(solution)/shard_map/concatenate | solution.py:149
  1093.3 12.3 gather_fusion.3
  1116.1 14.6 %reshape.611 = f32[64,6,4,4,512]{4,3,2,1,0:T(4,128)} reshape(f32[384,16,512]{2,1,0:T(8,128)} %broadcast_select_fusion) | data formatting | bytes 25165824 | tf_op jit(solution)/shard_map/reshape | solution.py:157
  1130.7 13.8 %fusion = f32[64,6,4,4,512]{4,0,3,2,1:T(8,128)S(1)} fusion(f32[64,6,4,4,512]{4,0,3,2,1:T(8,128)} %copy-done.6, f32[64,6,4,4,512]{4,3,2,1,0:T(4,128)} %reshape.611, f32[64,6,512]{2,0,1:T(8,128)S(1)} %copy-done.12), kind=kLoop, calls=%fused_computation.7 | loop fusion | flops 6291456 | bytes 38535168 | tf_op jit(solution)/shard_map/mul | solution.py:101
  1164.6 48.3 %all-to-all-done.5 = f32[8,64,8,512]{3,2,1,0:T(8,128)} async-done(((f32[8,64,8,512]{3,2,1,0:T(8,128)}), f32[8,64,8,512]{3,2,1,0:T(8,128)}, u32[]{:S(2)}, u32[]{:S(2)}) %all-to-all-start.5) | async-done | bytes 8388640 | tf_op jit(solution)/shard_map/all_to_all | solution.py:163
  1218.7 44.3 %fusion.12 = f32[64,64,512]{2,0,1:T(8,128)} fusion(f32[64,64,512]{2,0,1:T(8,128)} %fusion.27, f32[64,1,64,512]{3,2,1,0:T(8,128)} %get-tuple-element.9, f32[64,1,64,512]{3,2,1,0:T(8,128)} %get-tuple-element.8, f32[64,1,64,512]{3,2,1,0:T(8,128)} %get-tuple-element.6, f32[64,4,4,4,512]{4,0,3,2,1:T(8,128)S(1)} %copy-done.7, ...), kind=kLoop, calls=%fused_computation.24 | loop fusion | flops 27262976 | bytes 67518464 | tf_op jit(solution)/shard_map/add | solution.py:177
  1262.9 11.6 copy.193
  (570 shorter events, 527.4 us)
Async XLA Ops:
  11.6 134.0 %copy-start.31 = (s32[1,4,48]{2,1,0:T(4,128)S(1)}, s32[1,4,48]{2,1,0:T(4,128)}, u32[]{:S(2)}) copy-start(s32[1,4,48]{2,1,0:T(4,128)} %param.20) | copy-start | bytes 2308
  11.6 191.0 %all-to-all-start.1 = ((f32[64,64,512]{2,0,1:T(8,128)}), f32[64,64,512]{2,0,1:T(8,128)}, u32[]{:S(2)}, u32[]{:S(2)}) async-start(f32[64,64,512]{2,0,1:T(8,128)} %copy.192), calls=%async_computation.1 | async-start | bytes 16777216 | tf_op jit(solution)/shard_map/all_to_all | solution.py:169
  202.6 171.5 %all-to-all-start = ((f32[4,48,16,512]{3,2,1,0:T(8,128)}), f32[4,48,16,512]{3,2,1,0:T(8,128)}, u32[]{:S(2)}, u32[]{:S(2)}) async-start(f32[4,48,16,512]{3,2,1,0:T(8,128)} %broadcast_select_fusion.3), calls=%async_computation | async-start | bytes 12582912 | tf_op jit(solution)/shard_map/all_to_all | solution.py:148
  208.0 30.2 %slice-start = ((s8[12582912]{0:T(1024)(128)(4,1)}), s8[4194304]{0:T(1024)(128)(4,1)S(1)}, s32[]{:S(2)}) async-start(s8[12582912]{0:T(1024)(128)(4,1)} %bitcast.1818), calls=%async_computation.6 | async-start | bytes 8388608
  216.5 118.0 %copy-start = (f32[64,8,8,512]{3,2,1,0:T(8,128)}, f32[64,8,8,512]{3,2,1,0:T(8,128)S(1)}, u32[]{:S(2)}) copy-start(f32[64,8,8,512]{3,2,1,0:T(8,128)S(1)} %copy.168) | copy-start | bytes 25165828
  374.1 189.0 %all-to-all-start.2 = ((f32[8,64,8,512]{3,2,1,0:T(8,128)}), f32[8,64,8,512]{3,2,1,0:T(8,128)}, u32[]{:S(2)}, u32[]{:S(2)}) async-start(f32[8,64,8,512]{3,2,1,0:T(8,128)} %fusion.113), calls=%async_computation.2 | async-start | bytes 16777216 | tf_op jit(solution)/shard_map/all_to_all | solution.py:163
  379.3 191.9 %copy-start.20 = (f32[64,64]{0,1:T(8,128)}, f32[64,64]{0,1:T(8,128)S(1)}, u32[]{:S(2)}) copy-start(f32[64,64]{0,1:T(8,128)S(1)} %copy.166) | copy-start | bytes 49156
  379.7 44.0 %copy-start.24 = (f32[577]{0:T(1024)}, f32[577]{0:T(1024)S(1)}, u32[]{:S(2)}) copy-start(f32[577]{0:T(1024)S(1)} %pad.59.clone) | copy-start | bytes 6928
  380.1 96.9 %copy-start.11 = (f32[64,6,512]{2,0,1:T(8,128)}, f32[64,6,512]{2,0,1:T(8,128)S(1)}, u32[]{:S(2)}) copy-start(f32[64,6,512]{2,0,1:T(8,128)S(1)} %fusion.122) | copy-start | bytes 2359300
  380.1 59.6 %copy-start.27 = (s32[1024]{0:T(1024)}, s32[1024]{0:T(1024)S(1)}, u32[]{:S(2)}) copy-start(s32[1024]{0:T(1024)S(1)} %pad_clamp_fusion) | copy-start | bytes 12292
  380.1 71.9 %copy-start.32 = (pred[384]{0:T(512)(128)(4,1)}, pred[384]{0:T(512)(128)(4,1)S(1)}, u32[]{:S(2)}) copy-start(pred[384]{0:T(512)(128)(4,1)S(1)} %compare_and_fusion) | copy-start | bytes 1156
  380.2 191.0 %copy-start.14 = (f32[64,512]{1,0:T(8,128)}, f32[64,512]{1,0:T(8,128)S(1)}, u32[]{:S(2)}) copy-start(f32[64,512]{1,0:T(8,128)S(1)} %get-tuple-element.23) | copy-start | bytes 393220
  380.2 191.0 %copy-start.16 = (f32[64,512]{1,0:T(8,128)}, f32[64,512]{1,0:T(8,128)S(1)}, u32[]{:S(2)}) copy-start(f32[64,512]{1,0:T(8,128)S(1)} %get-tuple-element.24) | copy-start | bytes 393220
  380.2 191.0 %copy-start.18 = (f32[64,512]{1,0:T(8,128)}, f32[64,512]{1,0:T(8,128)S(1)}, u32[]{:S(2)}) copy-start(f32[64,512]{1,0:T(8,128)S(1)} %get-tuple-element.25) | copy-start | bytes 393220
  623.5 188.8 %all-to-all-start.4 = ((f32[64,64,512]{2,0,1:T(8,128)}), f32[64,64,512]{2,0,1:T(8,128)}, u32[]{:S(2)}, u32[]{:S(2)}) async-start(f32[64,64,512]{2,0,1:T(8,128)} %fusion.27), calls=%async_computation.4 | async-start | bytes 16777216 | tf_op jit(solution)/shard_map/all_to_all | solution.py:169
  812.3 211.6 %all-to-all-start.3 = ((f32[4,48,16,512]{3,2,1,0:T(8,128)}), f32[4,48,16,512]{3,2,1,0:T(8,128)}, u32[]{:S(2)}, u32[]{:S(2)}) async-start(f32[4,48,16,512]{3,2,1,0:T(8,128)} %broadcast_select_fusion.2), calls=%async_computation.3 | async-start | bytes 12582912 | tf_op jit(solution)/shard_map/all_to_all | solution.py:148
  834.5 132.1 %copy-start.1 = (f32[64,8,8,512]{3,1,2,0:T(8,128)}, f32[64,8,8,512]{3,1,2,0:T(8,128)S(1)}, u32[]{:S(2)}) copy-start(f32[64,8,8,512]{3,1,2,0:T(8,128)S(1)} %copy.217) | copy-start | bytes 25165828
  834.5 50.0 %slice-start.3 = ((s8[12582912]{0:T(1024)(128)(4,1)}), s8[4194304]{0:T(1024)(128)(4,1)S(1)}, s32[]{:S(2)}) async-start(s8[12582912]{0:T(1024)(128)(4,1)} %bitcast.1820), calls=%async_computation.9 | async-start | bytes 8388608
  853.8 30.7 %slice-start.4 = ((s8[12582912]{0:T(1024)(128)(4,1)}), s8[4194304]{0:T(1024)(128)(4,1)S(1)}, s32[]{:S(2)}) async-start(s8[12582912]{0:T(1024)(128)(4,1)} %bitcast.1820), calls=%async_computation.10 | async-start | bytes 8388608
  1024.0 188.9 %all-to-all-start.5 = ((f32[8,64,8,512]{3,2,1,0:T(8,128)}), f32[8,64,8,512]{3,2,1,0:T(8,128)}, u32[]{:S(2)}, u32[]{:S(2)}) async-start(f32[8,64,8,512]{3,2,1,0:T(8,128)} %fusion.105), calls=%async_computation.5 | async-start | bytes 16777216 | tf_op jit(solution)/shard_map/all_to_all | solution.py:163
  1164.6 52.9 %copy-start.15 = (f32[64,512]{1,0:T(8,128)S(1)}, f32[64,512]{1,0:T(8,128)}, u32[]{:S(2)}) copy-start(f32[64,512]{1,0:T(8,128)} %copy-done.14) | copy-start | bytes 393220
  1164.6 52.9 %copy-start.17 = (f32[64,512]{1,0:T(8,128)S(1)}, f32[64,512]{1,0:T(8,128)}, u32[]{:S(2)}) copy-start(f32[64,512]{1,0:T(8,128)} %copy-done.16) | copy-start | bytes 393220
  1164.6 52.9 %copy-start.19 = (f32[64,512]{1,0:T(8,128)S(1)}, f32[64,512]{1,0:T(8,128)}, u32[]{:S(2)}) copy-start(f32[64,512]{1,0:T(8,128)} %copy-done.18) | copy-start | bytes 393220
  1164.6 53.0 %copy-start.21 = (f32[64,64]{0,1:T(8,128)S(1)}, f32[64,64]{0,1:T(8,128)}, u32[]{:S(2)}) copy-start(f32[64,64]{0,1:T(8,128)} %copy-done.20) | copy-start | bytes 49156
  (29 other events, 259.7 us)
